TPU v7x, 256 devices: a whole 4x4x8 slice. The times are simulated.
256 devices in a mesh: grp: 16 (over x, z_lo, core), row: 4 (over z_hi), col: 4 (over y).
Axes of the slice: x: 4, y: 4, z: 8 (z_hi: 4, z_lo: 2; z = z_hi * 2 + z_lo), core: 2. Of those that a mesh axis runs over, the one named last changes fastest.
Arguments:
- volume: float32 [32, 32, 32, 512], P(None, 'grp', 'row', 'col'), may hold values from -6 to 6
- forcing: float32 [32, 32, 32, 512], P(None, 'grp', 'row', 'col'), may hold values from -6 to 6
- medium: float32 [2, 32, 32, 512], P(None, 'grp', 'row', 'col'), may hold values from 0.5 to 3
- points: float32 [3, 32768], P(None, ('grp', 'row', 'col')), may hold values from 0 to 4
- weights: float32 [32768], P(('grp', 'row', 'col')), may hold values from 0.05 to 0.5
- cell_map: int32 [32768], P(('grp', 'row', 'col')), may hold values from 0 to 2047
- near_list: int32 [256, 256], replicated, may hold values from 0 to 1, as said below
Outputs:
- new_volume: float32 [32, 32, 32, 512], P(None, 'grp', 'row', 'col')
- potential: float32 [32, 32768], P(None, ('grp', 'row', 'col'))
Inputs may be any that keep to these rules, and one draw needn't show every extreme that they name: cell_map[p] numbers a cell of tile p // 128 in row-major order of the tile's 2 x 8 x 128 cells. near_list[i, j] = 1 lists cluster j as near to cluster i; every cluster lists itself, and how many clusters a cluster lists differs from cluster to cluster.
All inputs are finite; a program needn't handle non-finite values.
Results may differ from a plain program's by a relative error of at most 0.0041.
Values may be sent and summed in bfloat16 or wider, within the bound.
No kernel may reach another device: no remote copies, remote signals or barrier semaphores. Data moves between devices by JAX's collectives and lax.ppermute only.
A program may use at most 64 MiB of HBM per device.

v0:
```python
import jax
import jax.numpy as jnp
from jax import lax
from jax.sharding import PartitionSpec as P

RHS = 16
CX = 2
CY = 8
CZ = 128
CH = 32
FOUR_PI = 4.0 * 3.141592653589793
WAVENUMBER = 10.0
SOFTENING = 0.01
RELAX_RATE = 0.8
COUPLING = 0.5
CONTRACT = (((1,), (1,)), ((), ()))


def padded_2(x, sides, width):
    for axis, dim in sides:
        size, length = (lax.axis_size(axis), x.shape[dim])
        up = [(i, (i + 1) % size) for i in range(size - 1)]
        down = [(j, i) for i, j in up]
        last = lax.slice_in_dim(x, length - width, length, axis=dim)
        first = lax.slice_in_dim(x, 0, width, axis=dim)
        before = lax.ppermute(last, axis, up)
        after = lax.ppermute(first, axis, down)
        x = jnp.concatenate([before, x, after], axis=dim)
    return x


def helmholtz(volume, medium):
    padded = padded_2(volume, (("grp", 1), ("row", 2), ("col", 3)), 1)
    beside = padded[:, 2:, 1:-1, 1:-1] + padded[:, :-2, 1:-1, 1:-1]
    beside = beside + padded[:, 1:-1, 2:, 1:-1] + padded[:, 1:-1, :-2, 1:-1]
    beside = beside + padded[:, 1:-1, 1:-1, 2:] + padded[:, 1:-1, 1:-1, :-2]
    laplace = 6.0 * volume - beside
    real_in = volume[:RHS]
    imag_in = volume[RHS:]
    real_out = laplace[:RHS] - medium[0] * real_in + medium[1] * imag_in
    imag_out = laplace[RHS:] - medium[0] * imag_in - medium[1] * real_in
    return jnp.concatenate([real_out, imag_out], 0)


def kernel_tiles(targets, sources, listed):
    delta_x = targets[0][:, None] - sources[0][None, :]
    delta_y = targets[1][:, None] - sources[1][None, :]
    delta_z = targets[2][:, None] - sources[2][None, :]
    distance = jnp.sqrt(delta_x * delta_x + delta_y * delta_y + delta_z * delta_z + SOFTENING)
    factor = listed / (FOUR_PI * distance)
    tile_real = (jnp.cos(WAVENUMBER * distance) * factor).astype(jnp.bfloat16)
    tile_imag = (jnp.sin(WAVENUMBER * distance) * factor).astype(jnp.bfloat16)
    return (tile_real, tile_imag)


def complex_product(real_sum, imag_sum):
    return jnp.concatenate([real_sum[:RHS] - imag_sum[RHS:], real_sum[RHS:] + imag_sum[:RHS]], 0)


def block_clusters(clusters, cluster_size, limit):
    chosen = 1
    for trial in range(1, clusters + 1):
        if clusters % trial == 0 and trial * cluster_size <= limit:
            chosen = trial
    return chosen


def on_device(volume, forcing, medium, points, weights, cell_map, near_list):
    residual = forcing - helmholtz(volume, medium)
    relaxed = volume + RELAX_RATE * residual / (6.0 - medium[0])[None]
    flat = relaxed.reshape(CH, CX * CY * CZ)
    traces = (jnp.take(flat, cell_map, axis=1) * weights[None, :]).astype(jnp.bfloat16)
    group_count = lax.axis_size("grp") * lax.axis_size("row")
    column_count = lax.axis_size("col")
    group_index = lax.axis_index("grp") * lax.axis_size("row") + lax.axis_index("row")
    column_index = lax.axis_index("col")
    near_blocks = near_list.reshape(group_count, column_count, group_count, column_count)
    cluster = points.shape[1]
    own_cols = lax.dynamic_index_in_dim(near_blocks, column_index, 1, keepdims=False)
    own_cols = lax.dynamic_index_in_dim(own_cols, group_index, 1, keepdims=False)
    targets = lax.all_gather(points, ("grp", "row"), axis=1, tiled=True)
    sources = lax.all_gather(points, "col", axis=1, tiled=True)
    source_traces = lax.all_gather(traces, "col", axis=1, tiled=True)
    target_count = targets.shape[1]
    source_count = sources.shape[1]
    step_clusters = block_clusters(group_count, cluster, 1024)
    block_points = step_clusters * cluster

    def one_block(turn, partial_value):
        begin = turn * block_points
        block_targets = lax.dynamic_slice_in_dim(targets, begin, block_points, 1)
        flags = lax.dynamic_slice_in_dim(own_cols, turn * step_clusters, step_clusters, 0)
        listed = jnp.broadcast_to(
            flags[:, None, :, None].astype(jnp.float32),
            (step_clusters, cluster, column_count, cluster),
        )
        listed = listed.reshape(block_points, source_count)
        tile_real, tile_imag = kernel_tiles(block_targets, sources, listed)
        real_part = lax.dot_general(
            source_traces, tile_real, CONTRACT, preferred_element_type=jnp.float32
        )
        imag_part = lax.dot_general(
            source_traces, tile_imag, CONTRACT, preferred_element_type=jnp.float32
        )
        return lax.dynamic_update_slice_in_dim(
            partial_value, complex_product(real_part, imag_part), begin, 1
        )

    partial_value = lax.fori_loop(
        0, group_count // step_clusters, one_block, jnp.zeros((CH, target_count), jnp.float32)
    )
    potential = lax.psum_scatter(partial_value, ("grp", "row"), scatter_dimension=1, tiled=True)
    spread = jnp.zeros((CH, CX * CY * CZ), jnp.float32).at[:, cell_map].add(potential)
    new_volume = relaxed + COUPLING * spread.reshape(relaxed.shape)
    return (new_volume, potential)


def solution(mesh):
    return jax.shard_map(
        on_device,
        mesh=mesh,
        in_specs=(
            P(None, "grp", "row", "col"),
            P(None, "grp", "row", "col"),
            P(None, "grp", "row", "col"),
            P(None, ("grp", "row", "col")),
            P(("grp", "row", "col")),
            P(("grp", "row", "col")),
            P(),
        ),
        out_specs=(P(None, "grp", "row", "col"), P(None, ("grp", "row", "col"))),
        check_vma=False,
    )
```

profile of v0, /device:TPU:24, one launch (start us, length us, event | category | flops | bytes accessed | tf_op | source)
XLA Modules:
  0.0 649.2 jit_solution(6016588470859238868)
XLA Ops:
  7.2 1.0 fusion.19
  8.2 1.7 collective-permute-start.1
  10.0 1.3 collective-permute-start
  11.3 1.3 subtract_bitcast_fusion
  13.2 1.2 compare_and_fusion
  14.5 10.9 %reshape.33 = s32[64,4,64,4]{3,2,1,0:T(8,128)} reshape(s32[256,256]{1,0:T(8,128)} %param.15) | data formatting | bytes 524288 | tf_op jit(solution)/shard_map/reshape | solution.py:77
  25.4 1.6 constant_dynamic-slice_fusion.1
  28.0 1.3 collective-permute-start.2
  29.3 5.8 collective-permute-start.3
  37.9 3.2 collective-permute-start.4
  41.1 1.3 collective-permute-start.5
  42.4 140.7 %all_gather.9 = f32[3,8192]{1,0:T(4,128)} all-gather(f32[3,128]{1,0:T(4,128)S(1)} %copy-done.7), channel_id=1, replica_groups=mesh['grp'=16,'row'=4,'col'=4] {'grp','row'}, dimensions={1}, use_global_device_ids=true | all-gather | bytes 99840 | tf_op jit(solution)/shard_map/all_gather | solution.py:81
  185.3 10.3 %all_gather.10 = f32[3,512]{1,0:T(4,128)S(1)} all-gather(f32[3,128]{1,0:T(4,128)} %param.12), channel_id=1, replica_groups=mesh['grp'=16,'row'=4,'col'=4] {'col'}, dimensions={1}, use_global_device_ids=true | all-gather | bytes 7680 | tf_op jit(solution)/shard_map/all_gather | solution.py:82
  195.7 2.3 copy.89
  198.0 2.3 copy.90
  200.2 2.9 fusion.7
  203.1 1.3 fusion.5
  206.7 12.0 %all_gather.11 = bf16[32,512]{0,1:T(8,128)(2,1)S(1)} all-gather(bf16[32,128]{0,1:T(8,128)(2,1)S(1)} %fusion.16), channel_id=1, replica_groups=mesh['grp'=16,'row'=4,'col'=4] {'col'}, dimensions={1}, use_global_device_ids=true | all-gather | bytes 40960 | tf_op jit(solution)/shard_map/all_gather | solution.py:83
  218.8 158.8 %while.13 = (s32[]{:T(128)}, f32[32,8192]{1,0:T(8,128)S(1)}, f32[3,8192]{1,0:T(4,128)}, f32[3,512]{1,0:T(4,128)S(1)}, s32[64,4]{0,1:T(4,128)S(1)}, /*index=5*/bf...) while((s32[]{:T(128)}, f32[32,8192]{1,0:T(8,128)S(1)}, ...), condition=%wide.region_1.2_spmd, body=%wide.region_0.1_spmd.sunk | while | flops 85524528 | bytes 11561869 | solution.py:109
  219.0 0.9 constant_dynamic-slice_fusion.3
  220.5 1.4 bitcast_divide_fusion.2
  221.8 8.4 %convolution_bitcast_fusion.5 = f32[32,1024]{1,0:T(8,128)S(1)} fusion(bf16[32,512]{1,0:T(8,128)(2,1)S(1)} %get-tuple-element.270, f32[1024,512]{1,0:T(8,128)S(1)} %bitcast_divide_fusion.2, f32[512]{0:T(512)S(1)} %bitcast.68, f32[1024]{0:T(1024)S(1)} %bitcast.62, f32[512]{0:T(512)S(1)} %bitcast.71, f32[1024]{0:T(1024)S(1)} %bitcast.59, ...), kind=kOutput, calls=%fused_computation.7.clone.1 | convolution fusion | flops 39845888 | bytes 2279424 | tf_op jit(solution)/shard_map/while/body/eval_jaxpr/dot_general | solution.py:99
  230.2 8.5 %convolution_bitcast_fusion.4 = f32[32,1024]{1,0:T(8,128)S(1)} fusion(bf16[32,512]{1,0:T(8,128)(2,1)S(1)} %get-tuple-element.270, f32[1024,512]{1,0:T(8,128)S(1)} %bitcast_divide_fusion.2, f32[512]{0:T(512)S(1)} %bitcast.69, f32[1024]{0:T(1024)S(1)} %bitcast.63, f32[512]{0:T(512)S(1)} %bitcast.72, f32[1024]{0:T(1024)S(1)} %bitcast.60, ...), kind=kOutput, calls=%fused_computation.6.clone.1 | convolution fusion | flops 39845888 | bytes 2279424 | tf_op jit(solution)/shard_map/while/body/eval_jaxpr/dot_general | solution.py:102
  240.3 1.4 bitcast_divide_fusion.2
  241.7 8.4 %convolution_bitcast_fusion.5 = f32[32,1024]{1,0:T(8,128)S(1)} fusion(bf16[32,512]{1,0:T(8,128)(2,1)S(1)} %get-tuple-element.270, f32[1024,512]{1,0:T(8,128)S(1)} %bitcast_divide_fusion.2, f32[512]{0:T(512)S(1)} %bitcast.68, f32[1024]{0:T(1024)S(1)} %bitcast.62, f32[512]{0:T(512)S(1)} %bitcast.71, f32[1024]{0:T(1024)S(1)} %bitcast.59, ...), kind=kOutput, calls=%fused_computation.7.clone.1 | convolution fusion | flops 39845888 | bytes 2279424 | tf_op jit(solution)/shard_map/while/body/eval_jaxpr/dot_general | solution.py:99
  250.1 8.5 %convolution_bitcast_fusion.4 = f32[32,1024]{1,0:T(8,128)S(1)} fusion(bf16[32,512]{1,0:T(8,128)(2,1)S(1)} %get-tuple-element.270, f32[1024,512]{1,0:T(8,128)S(1)} %bitcast_divide_fusion.2, f32[512]{0:T(512)S(1)} %bitcast.69, f32[1024]{0:T(1024)S(1)} %bitcast.63, f32[512]{0:T(512)S(1)} %bitcast.72, f32[1024]{0:T(1024)S(1)} %bitcast.60, ...), kind=kOutput, calls=%fused_computation.6.clone.1 | convolution fusion | flops 39845888 | bytes 2279424 | tf_op jit(solution)/shard_map/while/body/eval_jaxpr/dot_general | solution.py:102
  258.7 0.9 constant_dynamic-slice_fusion.3
  260.1 1.4 bitcast_divide_fusion.2
  261.5 8.4 %convolution_bitcast_fusion.5 = f32[32,1024]{1,0:T(8,128)S(1)} fusion(bf16[32,512]{1,0:T(8,128)(2,1)S(1)} %get-tuple-element.270, f32[1024,512]{1,0:T(8,128)S(1)} %bitcast_divide_fusion.2, f32[512]{0:T(512)S(1)} %bitcast.68, f32[1024]{0:T(1024)S(1)} %bitcast.62, f32[512]{0:T(512)S(1)} %bitcast.71, f32[1024]{0:T(1024)S(1)} %bitcast.59, ...), kind=kOutput, calls=%fused_computation.7.clone.1 | convolution fusion | flops 39845888 | bytes 2279424 | tf_op jit(solution)/shard_map/while/body/eval_jaxpr/dot_general | solution.py:99
  269.9 8.5 %convolution_bitcast_fusion.4 = f32[32,1024]{1,0:T(8,128)S(1)} fusion(bf16[32,512]{1,0:T(8,128)(2,1)S(1)} %get-tuple-element.270, f32[1024,512]{1,0:T(8,128)S(1)} %bitcast_divide_fusion.2, f32[512]{0:T(512)S(1)} %bitcast.69, f32[1024]{0:T(1024)S(1)} %bitcast.63, f32[512]{0:T(512)S(1)} %bitcast.72, f32[1024]{0:T(1024)S(1)} %bitcast.60, ...), kind=kOutput, calls=%fused_computation.6.clone.1 | convolution fusion | flops 39845888 | bytes 2279424 | tf_op jit(solution)/shard_map/while/body/eval_jaxpr/dot_general | solution.py:102
  280.0 1.4 bitcast_divide_fusion.2
  281.4 8.4 %convolution_bitcast_fusion.5 = f32[32,1024]{1,0:T(8,128)S(1)} fusion(bf16[32,512]{1,0:T(8,128)(2,1)S(1)} %get-tuple-element.270, f32[1024,512]{1,0:T(8,128)S(1)} %bitcast_divide_fusion.2, f32[512]{0:T(512)S(1)} %bitcast.68, f32[1024]{0:T(1024)S(1)} %bitcast.62, f32[512]{0:T(512)S(1)} %bitcast.71, f32[1024]{0:T(1024)S(1)} %bitcast.59, ...), kind=kOutput, calls=%fused_computation.7.clone.1 | convolution fusion | flops 39845888 | bytes 2279424 | tf_op jit(solution)/shard_map/while/body/eval_jaxpr/dot_general | solution.py:99
  289.8 8.5 %convolution_bitcast_fusion.4 = f32[32,1024]{1,0:T(8,128)S(1)} fusion(bf16[32,512]{1,0:T(8,128)(2,1)S(1)} %get-tuple-element.270, f32[1024,512]{1,0:T(8,128)S(1)} %bitcast_divide_fusion.2, f32[512]{0:T(512)S(1)} %bitcast.69, f32[1024]{0:T(1024)S(1)} %bitcast.63, f32[512]{0:T(512)S(1)} %bitcast.72, f32[1024]{0:T(1024)S(1)} %bitcast.60, ...), kind=kOutput, calls=%fused_computation.6.clone.1 | convolution fusion | flops 39845888 | bytes 2279424 | tf_op jit(solution)/shard_map/while/body/eval_jaxpr/dot_general | solution.py:102
  299.8 1.4 bitcast_divide_fusion.2
  301.2 8.4 %convolution_bitcast_fusion.5 = f32[32,1024]{1,0:T(8,128)S(1)} fusion(bf16[32,512]{1,0:T(8,128)(2,1)S(1)} %get-tuple-element.270, f32[1024,512]{1,0:T(8,128)S(1)} %bitcast_divide_fusion.2, f32[512]{0:T(512)S(1)} %bitcast.68, f32[1024]{0:T(1024)S(1)} %bitcast.62, f32[512]{0:T(512)S(1)} %bitcast.71, f32[1024]{0:T(1024)S(1)} %bitcast.59, ...), kind=kOutput, calls=%fused_computation.7.clone.1 | convolution fusion | flops 39845888 | bytes 2279424 | tf_op jit(solution)/shard_map/while/body/eval_jaxpr/dot_general | solution.py:99
  309.6 8.5 %convolution_bitcast_fusion.4 = f32[32,1024]{1,0:T(8,128)S(1)} fusion(bf16[32,512]{1,0:T(8,128)(2,1)S(1)} %get-tuple-element.270, f32[1024,512]{1,0:T(8,128)S(1)} %bitcast_divide_fusion.2, f32[512]{0:T(512)S(1)} %bitcast.69, f32[1024]{0:T(1024)S(1)} %bitcast.63, f32[512]{0:T(512)S(1)} %bitcast.72, f32[1024]{0:T(1024)S(1)} %bitcast.60, ...), kind=kOutput, calls=%fused_computation.6.clone.1 | convolution fusion | flops 39845888 | bytes 2279424 | tf_op jit(solution)/shard_map/while/body/eval_jaxpr/dot_general | solution.py:102
  319.6 1.4 bitcast_divide_fusion.2
  321.0 8.4 %convolution_bitcast_fusion.5 = f32[32,1024]{1,0:T(8,128)S(1)} fusion(bf16[32,512]{1,0:T(8,128)(2,1)S(1)} %get-tuple-element.270, f32[1024,512]{1,0:T(8,128)S(1)} %bitcast_divide_fusion.2, f32[512]{0:T(512)S(1)} %bitcast.68, f32[1024]{0:T(1024)S(1)} %bitcast.62, f32[512]{0:T(512)S(1)} %bitcast.71, f32[1024]{0:T(1024)S(1)} %bitcast.59, ...), kind=kOutput, calls=%fused_computation.7.clone.1 | convolution fusion | flops 39845888 | bytes 2279424 | tf_op jit(solution)/shard_map/while/body/eval_jaxpr/dot_general | solution.py:99
  329.4 8.5 %convolution_bitcast_fusion.4 = f32[32,1024]{1,0:T(8,128)S(1)} fusion(bf16[32,512]{1,0:T(8,128)(2,1)S(1)} %get-tuple-element.270, f32[1024,512]{1,0:T(8,128)S(1)} %bitcast_divide_fusion.2, f32[512]{0:T(512)S(1)} %bitcast.69, f32[1024]{0:T(1024)S(1)} %bitcast.63, f32[512]{0:T(512)S(1)} %bitcast.72, f32[1024]{0:T(1024)S(1)} %bitcast.60, ...), kind=kOutput, calls=%fused_computation.6.clone.1 | convolution fusion | flops 39845888 | bytes 2279424 | tf_op jit(solution)/shard_map/while/body/eval_jaxpr/dot_general | solution.py:102
  339.4 1.4 bitcast_divide_fusion.2
  340.8 8.4 %convolution_bitcast_fusion.5 = f32[32,1024]{1,0:T(8,128)S(1)} fusion(bf16[32,512]{1,0:T(8,128)(2,1)S(1)} %get-tuple-element.270, f32[1024,512]{1,0:T(8,128)S(1)} %bitcast_divide_fusion.2, f32[512]{0:T(512)S(1)} %bitcast.68, f32[1024]{0:T(1024)S(1)} %bitcast.62, f32[512]{0:T(512)S(1)} %bitcast.71, f32[1024]{0:T(1024)S(1)} %bitcast.59, ...), kind=kOutput, calls=%fused_computation.7.clone.1 | convolution fusion | flops 39845888 | bytes 2279424 | tf_op jit(solution)/shard_map/while/body/eval_jaxpr/dot_general | solution.py:99
  349.2 8.5 %convolution_bitcast_fusion.4 = f32[32,1024]{1,0:T(8,128)S(1)} fusion(bf16[32,512]{1,0:T(8,128)(2,1)S(1)} %get-tuple-element.270, f32[1024,512]{1,0:T(8,128)S(1)} %bitcast_divide_fusion.2, f32[512]{0:T(512)S(1)} %bitcast.69, f32[1024]{0:T(1024)S(1)} %bitcast.63, f32[512]{0:T(512)S(1)} %bitcast.72, f32[1024]{0:T(1024)S(1)} %bitcast.60, ...), kind=kOutput, calls=%fused_computation.6.clone.1 | convolution fusion | flops 39845888 | bytes 2279424 | tf_op jit(solution)/shard_map/while/body/eval_jaxpr/dot_general | solution.py:102
  359.3 1.4 bitcast_divide_fusion.2
  360.7 8.4 %convolution_bitcast_fusion.5 = f32[32,1024]{1,0:T(8,128)S(1)} fusion(bf16[32,512]{1,0:T(8,128)(2,1)S(1)} %get-tuple-element.270, f32[1024,512]{1,0:T(8,128)S(1)} %bitcast_divide_fusion.2, f32[512]{0:T(512)S(1)} %bitcast.68, f32[1024]{0:T(1024)S(1)} %bitcast.62, f32[512]{0:T(512)S(1)} %bitcast.71, f32[1024]{0:T(1024)S(1)} %bitcast.59, ...), kind=kOutput, calls=%fused_computation.7.clone.1 | convolution fusion | flops 39845888 | bytes 2279424 | tf_op jit(solution)/shard_map/while/body/eval_jaxpr/dot_general | solution.py:99
  369.1 8.5 %convolution_bitcast_fusion.4 = f32[32,1024]{1,0:T(8,128)S(1)} fusion(bf16[32,512]{1,0:T(8,128)(2,1)S(1)} %get-tuple-element.270, f32[1024,512]{1,0:T(8,128)S(1)} %bitcast_divide_fusion.2, f32[512]{0:T(512)S(1)} %bitcast.69, f32[1024]{0:T(1024)S(1)} %bitcast.63, f32[512]{0:T(512)S(1)} %bitcast.72, f32[1024]{0:T(1024)S(1)} %bitcast.60, ...), kind=kOutput, calls=%fused_computation.6.clone.1 | convolution fusion | flops 39845888 | bytes 2279424 | tf_op jit(solution)/shard_map/while/body/eval_jaxpr/dot_general | solution.py:102
  377.7 1.0 copy-done.1
  378.7 260.3 %reduce-scatter.2.cloned.1.call-done = f32[32,128]{1,0:T(8,128)} async-done(((f32[32,8192]{1,0:T(8,128)}), f32[32,128]{1,0:T(8,128)}) %reduce-scatter.2.cloned.1.call-update) | async-done | bytes 16400 | tf_op jit(solution)/shard_map/reduce_scatter | solution.py:112
  639.8 1.4 scatter_custom_fusion
  (111 shorter events, 20.7 us)
Async XLA Ops:
  7.2 631.8 %reduce-scatter.2.cloned.1.call-start = ((), (), s32[]{:S(2)}) async-start(), calls=%async_computation.1 | async-start | bytes 1064960 | tf_op jit(solution)/shard_map/reduce_scatter | solution.py:112
  8.2 18.8 %collective-permute-start.1 = (f32[32,1,8,128]{3,2,1,0:T(8,128)S(1)}, f32[32,1,8,128]{3,2,1,0:T(8,128)S(1)}, u32[]{:S(2)}, u32[]{:S(2)}) collective-permute-start(f32[32,1,8,128]{3,2,1,0:T(8,128)S(1)} %get-tuple-element.180), channel_id=1, source_target_pairs={{0,16},{16,32},{32,48},{48,64},{64,80},{80,96},{96,112},{112,128},... | collective-permute-start | bytes 393224 | tf_op jit(solution)/shard_map/ppermute | solution.py:26
  10.0 17.0 %collective-permute-start = (f32[32,1,8,128]{3,2,1,0:T(8,128)S(1)}, f32[32,1,8,128]{3,2,1,0:T(8,128)S(1)}, u32[]{:S(2)}, u32[]{:S(2)}) collective-permute-start(f32[32,1,8,128]{3,2,1,0:T(8,128)S(1)} %get-tuple-element.179), channel_id=1, source_target_pairs={{16,0},{32,16},{48,32},{64,48},{80,64},{96,80},{112,96},{128,112},... | collective-permute-start | bytes 393224 | tf_op jit(solution)/shard_map/ppermute | solution.py:27
  13.2 21.9 %copy-start.10 = (s32[128]{0:T(128)}, s32[128]{0:T(128)S(1)}, u32[]{:S(2)}) copy-start(s32[128]{0:T(128)S(1)} %compare_select_fusion) | copy-start | bytes 1540
  14.5 12.5 %copy-start = (f32[32,2,8,128]{3,2,1,0:T(8,128)S(1)}, f32[32,2,8,128]{3,2,1,0:T(8,128)}, u32[]{:S(2)}) copy-start(f32[32,2,8,128]{3,2,1,0:T(8,128)} %param.9) | copy-start | bytes 786436
  28.0 8.6 %collective-permute-start.2 = (f32[32,4,1,128]{3,0,2,1:T(8,128)S(1)}, f32[32,4,1,128]{3,0,2,1:T(8,128)S(1)}, u32[]{:S(2)}, u32[]{:S(2)}) collective-permute-start(f32[32,4,1,128]{3,0,2,1:T(8,128)S(1)} %copy.91), channel_id=1, source_target_pairs={{4,0},{8,4},{12,8},{5,1},{9,5},{13,9},{6,2},{10,6},{14,10},{7,3},{... | collective-permute-start | bytes 196616 | tf_op jit(solution)/shard_map/ppermute | solution.py:27
  29.3 7.7 %collective-permute-start.3 = (f32[32,4,1,128]{3,0,2,1:T(8,128)S(1)}, f32[32,4,1,128]{3,0,2,1:T(8,128)S(1)}, u32[]{:S(2)}, u32[]{:S(2)}) collective-permute-start(f32[32,4,1,128]{3,0,2,1:T(8,128)S(1)} %copy.92), channel_id=1, source_target_pairs={{0,4},{4,8},{8,12},{1,5},{5,9},{9,13},{2,6},{6,10},{10,14},{3,7},{... | collective-permute-start | bytes 196616 | tf_op jit(solution)/shard_map/ppermute | solution.py:26
  36.5 5.9 copy-start.7
  36.7 5.7 copy-start.2
  37.1 5.3 copy-start.3
  37.9 162.4 %collective-permute-start.4 = (f32[32,4,10,1]{0,2,3,1:T(8,128)}, f32[32,4,10,1]{0,2,3,1:T(8,128)}, u32[]{:S(2)}, u32[]{:S(2)}) collective-permute-start(f32[32,4,10,1]{0,2,3,1:T(8,128)} %get-tuple-element.170), channel_id=1, source_target_pairs={{1,0},{2,1},{3,2},{5,4},{6,5},{7,6},{9,8},{10,9},{11,10},{13,12},{... | collective-permute-start | bytes 15368 | tf_op jit(solution)/shard_map/ppermute | solution.py:27
  41.1 159.1 %collective-permute-start.5 = (f32[32,4,10,1]{0,2,3,1:T(8,128)}, f32[32,4,10,1]{0,2,3,1:T(8,128)}, u32[]{:S(2)}, u32[]{:S(2)}) collective-permute-start(f32[32,4,10,1]{0,2,3,1:T(8,128)} %get-tuple-element.171), channel_id=1, source_target_pairs={{0,1},{1,2},{2,3},{4,5},{5,6},{6,7},{8,9},{9,10},{10,11},{12,13},{... | collective-permute-start | bytes 15368 | tf_op jit(solution)/shard_map/ppermute | solution.py:26
  200.2 2.9 copy-start.4
  204.4 1.0 copy-start.5
  204.4 0.9 copy-start.6
  204.8 1.8 copy-start.8
  204.8 1.8 copy-start.9
  377.6 1.0 copy-start.1
Sparse Core Ops, SparseCore 0:
  378.8 260.1 reduce-scatter.1
where the time goes:
time: 651 us; the launch traced here: 649 us
  waiting for transfers between devices  261 us (40%)
  blocking collectives  163 us (25%)
  matrix products  135 us (21%)
  local copies, waits for them, and re-layouts  36.5 us (6%)
  other arithmetic  23.8 us (4%)
  starting transfers between devices  14.7 us (2%)
  between operations  14.4 us (2%)
    reduce_scatter x1, waiting for transfers between devices, on_device(): lax.psum_scatter(partial_value, ('grp', 'row'), scatter_dimension=1, tile...  260 us
    all_gather x1, blocking collectives, on_device(): targets = lax.all_gather(points, ('grp', 'row'), axis=1, tiled=True)  141 us
    dot_general x8, matrix products, one_block(): lax.dot_general(source_traces, tile_imag, CONTRACT, preferred_element_typ...  68.1 us
    dot_general x8, matrix products, one_block(): lax.dot_general(source_traces, tile_real, CONTRACT, preferred_element_typ...  67.3 us
  transfers between devices with their start and end apart: 7, of which 2 were waited for; matrix products, arithmetic and copies ran while one was open for 4% of the time, Pallas kernels for 0%

commit v1 on v0

--- a/solution.py
+++ b/solution.py
@@ -78,7 +78,10 @@
     cluster = points.shape[1]
     own_cols = lax.dynamic_index_in_dim(near_blocks, column_index, 1, keepdims=False)
     own_cols = lax.dynamic_index_in_dim(own_cols, group_index, 1, keepdims=False)
-    targets = lax.all_gather(points, ("grp", "row"), axis=1, tiled=True)
+    count = lax.axis_size(("grp", "row"))
+    blocks = jnp.stack([points for _ in range(count)])
+    blocks = lax.all_to_all(blocks, ("grp", "row"), split_axis=0, concat_axis=0)
+    targets = jnp.concatenate(blocks, axis=1)
     sources = lax.all_gather(points, "col", axis=1, tiled=True)
     source_traces = lax.all_gather(traces, "col", axis=1, tiled=True)
     target_count = targets.shape[1]

time: 651 us -> 534 us (0.82)
  blocking collectives: 163 us -> 22.4 us
  starting transfers between devices: 14.7 us -> 30 us
  waiting for transfers between devices: 261 us -> 268 us
    all_gather x1 -> x0, blocking collectives: 141 us -> none  [on_device(): targets = lax.all_gather(points, ('grp', 'row'), axis=1, tiled=True)]
    all_to_all x0 -> x1, starting transfers between devices: none -> 15.6 us  [on_device(): blocks = lax.all_to_all(blocks, ('grp', 'row'), split_axis=0, concat_axis=0)]
    reduce_scatter x1, waiting for transfers between devices: 260 us -> 268 us  [on_device(): lax.psum_scatter(partial_value, ('grp', 'row'), scatter_dimension=1, tile...]
  transfers between devices with their start and end apart: 7 -> 8, of which waited for: 2 -> 1; matrix products, arithmetic and copies ran while one was open for 4% -> 6% of each run, Pallas kernels for 0% -> 0%
where the time goes in v1:
time: 534 us; the launch traced here: 533 us
  waiting for transfers between devices  268 us (50%)
  matrix products  135 us (25%)
  local copies, waits for them, and re-layouts  37.9 us (7%)
  starting transfers between devices  30 us (6%)
  other arithmetic  23.8 us (4%)
  blocking collectives  22.4 us (4%)
  between operations  14.4 us (3%)
    reduce_scatter x1, waiting for transfers between devices, on_device(): lax.psum_scatter(partial_value, ('grp', 'row'), scatter_dimension=1, tile...  268 us
    dot_general x8, matrix products, one_block(): lax.dot_general(source_traces, tile_imag, CONTRACT, preferred_element_typ...  68.1 us
    dot_general x8, matrix products, one_block(): lax.dot_general(source_traces, tile_real, CONTRACT, preferred_element_typ...  67.3 us
    all_to_all x1, starting transfers between devices, on_device(): blocks = lax.all_to_all(blocks, ('grp', 'row'), split_axis=0, concat_axis=0)  15.6 us
    all_gather x1, blocking collectives, on_device(): source_traces = lax.all_gather(traces, 'col', axis=1, tiled=True)  12.1 us
    div x8, other arithmetic, kernel_tiles(): factor = listed / (FOUR_PI * distance)  11 us
    reshape x1, local copies, waits for them, and re-layouts, on_device(): near_list.reshape(group_count, column_count, group_count, column_count)  10.9 us
  transfers between devices with their start and end apart: 8, of which 1 were waited for; matrix products, arithmetic and copies ran while one was open for 6% of the time, Pallas kernels for 0%

profile of v1, /device:TPU:24, one launch (start us, length us, event | category | flops | bytes accessed | tf_op | source)
XLA Modules:
  0.0 532.6 jit_solution(10772994141709278477)
XLA Ops:
  7.2 1.0 fusion.19
  8.2 1.7 collective-permute-start.1
  9.9 1.3 collective-permute-start
  11.2 1.4 stack.2
  12.6 15.6 %all-to-all-start = ((f32[64,3,128]{2,1,0:T(4,128)}), f32[64,3,128]{2,1,0:T(4,128)}, u32[]{:S(2)}, u32[]{:S(2)}) async-start(f32[64,3,128]{2,1,0:T(4,128)} %stack.2), calls=%async_computation | async-start | bytes 262144 | tf_op jit(solution)/shard_map/all_to_all | solution.py:83
  28.2 1.3 subtract_bitcast_fusion
  30.2 1.2 compare_and_fusion
  31.5 10.9 %reshape.43 = s32[64,4,64,4]{3,2,1,0:T(8,128)} reshape(s32[256,256]{1,0:T(8,128)} %param.15) | data formatting | bytes 524288 | tf_op jit(solution)/shard_map/reshape | solution.py:77
  43.4 1.3 collective-permute-start.2
  44.7 5.4 %collective-permute-start.3 = (f32[32,4,1,128]{3,0,2,1:T(8,128)S(1)}, f32[32,4,1,128]{3,0,2,1:T(8,128)S(1)}, u32[]{:S(2)}, u32[]{:S(2)}) collective-permute-start(f32[32,4,1,128]{3,0,2,1:T(8,128)S(1)} %copy.92), channel_id=1, source_target_pairs={{0,4},{4,8},{8,12},{1,5},{5,9},{9,13},{2,6},{6,10},{10,14},{3,7},{... | collective-permute-start | bytes 196616 | tf_op jit(solution)/shard_map/ppermute | solution.py:26
  50.2 1.6 constant_dynamic-slice_fusion.1
  53.6 3.2 collective-permute-start.4
  56.8 1.3 collective-permute-start.5
  60.9 10.3 %all_gather.6 = f32[3,512]{1,0:T(4,128)S(1)} all-gather(f32[3,128]{1,0:T(4,128)} %param.12), channel_id=1, replica_groups=mesh['grp'=16,'row'=4,'col'=4] {'col'}, dimensions={1}, use_global_device_ids=true | all-gather | bytes 7680 | tf_op jit(solution)/shard_map/all_gather | solution.py:85
  71.2 2.3 copy.89
  73.5 2.3 copy.90
  75.8 2.9 fusion.7
  78.7 1.3 fusion.5
  82.2 12.1 %all_gather.7 = bf16[32,512]{0,1:T(8,128)(2,1)S(1)} all-gather(bf16[32,128]{0,1:T(8,128)(2,1)S(1)} %fusion.16), channel_id=1, replica_groups=mesh['grp'=16,'row'=4,'col'=4] {'col'}, dimensions={1}, use_global_device_ids=true | all-gather | bytes 40960 | tf_op jit(solution)/shard_map/all_gather | solution.py:86
  94.5 158.8 %while.13 = (s32[]{:T(128)}, f32[32,8192]{1,0:T(8,128)S(1)}, f32[3,8192]{1,0:T(4,128)}, f32[3,512]{1,0:T(4,128)S(1)}, s32[64,4]{0,1:T(4,128)S(1)}, /*index=5*/bf...) while((s32[]{:T(128)}, f32[32,8192]{1,0:T(8,128)S(1)}, ...), condition=%wide.region_1.2_spmd, body=%wide.region_0.1_spmd.sunk | while | flops 85524528 | bytes 11561869 | solution.py:112
  96.1 1.4 bitcast_divide_fusion.2
  97.5 8.4 %convolution_bitcast_fusion.5 = f32[32,1024]{1,0:T(8,128)S(1)} fusion(bf16[32,512]{1,0:T(8,128)(2,1)S(1)} %get-tuple-element.270, f32[1024,512]{1,0:T(8,128)S(1)} %bitcast_divide_fusion.2, f32[512]{0:T(512)S(1)} %bitcast.71, f32[1024]{0:T(1024)S(1)} %bitcast.65, f32[512]{0:T(512)S(1)} %bitcast.74, f32[1024]{0:T(1024)S(1)} %bitcast.62, ...), kind=kOutput, calls=%fused_computation.7.clone.1 | convolution fusion | flops 39845888 | bytes 2279424 | tf_op jit(solution)/shard_map/while/body/eval_jaxpr/dot_general | solution.py:102
  105.9 8.5 %convolution_bitcast_fusion.4 = f32[32,1024]{1,0:T(8,128)S(1)} fusion(bf16[32,512]{1,0:T(8,128)(2,1)S(1)} %get-tuple-element.270, f32[1024,512]{1,0:T(8,128)S(1)} %bitcast_divide_fusion.2, f32[512]{0:T(512)S(1)} %bitcast.72, f32[1024]{0:T(1024)S(1)} %bitcast.66, f32[512]{0:T(512)S(1)} %bitcast.75, f32[1024]{0:T(1024)S(1)} %bitcast.63, ...), kind=kOutput, calls=%fused_computation.6.clone.1 | convolution fusion | flops 39845888 | bytes 2279424 | tf_op jit(solution)/shard_map/while/body/eval_jaxpr/dot_general | solution.py:105
  114.5 0.9 constant_dynamic-slice_fusion.3
  116.0 1.4 bitcast_divide_fusion.2
  117.3 8.4 %convolution_bitcast_fusion.5 = f32[32,1024]{1,0:T(8,128)S(1)} fusion(bf16[32,512]{1,0:T(8,128)(2,1)S(1)} %get-tuple-element.270, f32[1024,512]{1,0:T(8,128)S(1)} %bitcast_divide_fusion.2, f32[512]{0:T(512)S(1)} %bitcast.71, f32[1024]{0:T(1024)S(1)} %bitcast.65, f32[512]{0:T(512)S(1)} %bitcast.74, f32[1024]{0:T(1024)S(1)} %bitcast.62, ...), kind=kOutput, calls=%fused_computation.7.clone.1 | convolution fusion | flops 39845888 | bytes 2279424 | tf_op jit(solution)/shard_map/while/body/eval_jaxpr/dot_general | solution.py:102
  125.7 8.5 %convolution_bitcast_fusion.4 = f32[32,1024]{1,0:T(8,128)S(1)} fusion(bf16[32,512]{1,0:T(8,128)(2,1)S(1)} %get-tuple-element.270, f32[1024,512]{1,0:T(8,128)S(1)} %bitcast_divide_fusion.2, f32[512]{0:T(512)S(1)} %bitcast.72, f32[1024]{0:T(1024)S(1)} %bitcast.66, f32[512]{0:T(512)S(1)} %bitcast.75, f32[1024]{0:T(1024)S(1)} %bitcast.63, ...), kind=kOutput, calls=%fused_computation.6.clone.1 | convolution fusion | flops 39845888 | bytes 2279424 | tf_op jit(solution)/shard_map/while/body/eval_jaxpr/dot_general | solution.py:105
  135.8 1.4 bitcast_divide_fusion.2
  137.2 8.4 %convolution_bitcast_fusion.5 = f32[32,1024]{1,0:T(8,128)S(1)} fusion(bf16[32,512]{1,0:T(8,128)(2,1)S(1)} %get-tuple-element.270, f32[1024,512]{1,0:T(8,128)S(1)} %bitcast_divide_fusion.2, f32[512]{0:T(512)S(1)} %bitcast.71, f32[1024]{0:T(1024)S(1)} %bitcast.65, f32[512]{0:T(512)S(1)} %bitcast.74, f32[1024]{0:T(1024)S(1)} %bitcast.62, ...), kind=kOutput, calls=%fused_computation.7.clone.1 | convolution fusion | flops 39845888 | bytes 2279424 | tf_op jit(solution)/shard_map/while/body/eval_jaxpr/dot_general | solution.py:102
  145.6 8.5 %convolution_bitcast_fusion.4 = f32[32,1024]{1,0:T(8,128)S(1)} fusion(bf16[32,512]{1,0:T(8,128)(2,1)S(1)} %get-tuple-element.270, f32[1024,512]{1,0:T(8,128)S(1)} %bitcast_divide_fusion.2, f32[512]{0:T(512)S(1)} %bitcast.72, f32[1024]{0:T(1024)S(1)} %bitcast.66, f32[512]{0:T(512)S(1)} %bitcast.75, f32[1024]{0:T(1024)S(1)} %bitcast.63, ...), kind=kOutput, calls=%fused_computation.6.clone.1 | convolution fusion | flops 39845888 | bytes 2279424 | tf_op jit(solution)/shard_map/while/body/eval_jaxpr/dot_general | solution.py:105
  155.6 1.4 bitcast_divide_fusion.2
  157.0 8.4 %convolution_bitcast_fusion.5 = f32[32,1024]{1,0:T(8,128)S(1)} fusion(bf16[32,512]{1,0:T(8,128)(2,1)S(1)} %get-tuple-element.270, f32[1024,512]{1,0:T(8,128)S(1)} %bitcast_divide_fusion.2, f32[512]{0:T(512)S(1)} %bitcast.71, f32[1024]{0:T(1024)S(1)} %bitcast.65, f32[512]{0:T(512)S(1)} %bitcast.74, f32[1024]{0:T(1024)S(1)} %bitcast.62, ...), kind=kOutput, calls=%fused_computation.7.clone.1 | convolution fusion | flops 39845888 | bytes 2279424 | tf_op jit(solution)/shard_map/while/body/eval_jaxpr/dot_general | solution.py:102
  165.4 8.5 %convolution_bitcast_fusion.4 = f32[32,1024]{1,0:T(8,128)S(1)} fusion(bf16[32,512]{1,0:T(8,128)(2,1)S(1)} %get-tuple-element.270, f32[1024,512]{1,0:T(8,128)S(1)} %bitcast_divide_fusion.2, f32[512]{0:T(512)S(1)} %bitcast.72, f32[1024]{0:T(1024)S(1)} %bitcast.66, f32[512]{0:T(512)S(1)} %bitcast.75, f32[1024]{0:T(1024)S(1)} %bitcast.63, ...), kind=kOutput, calls=%fused_computation.6.clone.1 | convolution fusion | flops 39845888 | bytes 2279424 | tf_op jit(solution)/shard_map/while/body/eval_jaxpr/dot_general | solution.py:105
  175.4 1.4 bitcast_divide_fusion.2
  176.8 8.4 %convolution_bitcast_fusion.5 = f32[32,1024]{1,0:T(8,128)S(1)} fusion(bf16[32,512]{1,0:T(8,128)(2,1)S(1)} %get-tuple-element.270, f32[1024,512]{1,0:T(8,128)S(1)} %bitcast_divide_fusion.2, f32[512]{0:T(512)S(1)} %bitcast.71, f32[1024]{0:T(1024)S(1)} %bitcast.65, f32[512]{0:T(512)S(1)} %bitcast.74, f32[1024]{0:T(1024)S(1)} %bitcast.62, ...), kind=kOutput, calls=%fused_computation.7.clone.1 | convolution fusion | flops 39845888 | bytes 2279424 | tf_op jit(solution)/shard_map/while/body/eval_jaxpr/dot_general | solution.py:102
  185.2 8.5 %convolution_bitcast_fusion.4 = f32[32,1024]{1,0:T(8,128)S(1)} fusion(bf16[32,512]{1,0:T(8,128)(2,1)S(1)} %get-tuple-element.270, f32[1024,512]{1,0:T(8,128)S(1)} %bitcast_divide_fusion.2, f32[512]{0:T(512)S(1)} %bitcast.72, f32[1024]{0:T(1024)S(1)} %bitcast.66, f32[512]{0:T(512)S(1)} %bitcast.75, f32[1024]{0:T(1024)S(1)} %bitcast.63, ...), kind=kOutput, calls=%fused_computation.6.clone.1 | convolution fusion | flops 39845888 | bytes 2279424 | tf_op jit(solution)/shard_map/while/body/eval_jaxpr/dot_general | solution.py:105
  195.3 1.4 bitcast_divide_fusion.2
  196.7 8.4 %convolution_bitcast_fusion.5 = f32[32,1024]{1,0:T(8,128)S(1)} fusion(bf16[32,512]{1,0:T(8,128)(2,1)S(1)} %get-tuple-element.270, f32[1024,512]{1,0:T(8,128)S(1)} %bitcast_divide_fusion.2, f32[512]{0:T(512)S(1)} %bitcast.71, f32[1024]{0:T(1024)S(1)} %bitcast.65, f32[512]{0:T(512)S(1)} %bitcast.74, f32[1024]{0:T(1024)S(1)} %bitcast.62, ...), kind=kOutput, calls=%fused_computation.7.clone.1 | convolution fusion | flops 39845888 | bytes 2279424 | tf_op jit(solution)/shard_map/while/body/eval_jaxpr/dot_general | solution.py:102
  205.1 8.5 %convolution_bitcast_fusion.4 = f32[32,1024]{1,0:T(8,128)S(1)} fusion(bf16[32,512]{1,0:T(8,128)(2,1)S(1)} %get-tuple-element.270, f32[1024,512]{1,0:T(8,128)S(1)} %bitcast_divide_fusion.2, f32[512]{0:T(512)S(1)} %bitcast.72, f32[1024]{0:T(1024)S(1)} %bitcast.66, f32[512]{0:T(512)S(1)} %bitcast.75, f32[1024]{0:T(1024)S(1)} %bitcast.63, ...), kind=kOutput, calls=%fused_computation.6.clone.1 | convolution fusion | flops 39845888 | bytes 2279424 | tf_op jit(solution)/shard_map/while/body/eval_jaxpr/dot_general | solution.py:105
  215.1 1.4 bitcast_divide_fusion.2
  216.5 8.4 %convolution_bitcast_fusion.5 = f32[32,1024]{1,0:T(8,128)S(1)} fusion(bf16[32,512]{1,0:T(8,128)(2,1)S(1)} %get-tuple-element.270, f32[1024,512]{1,0:T(8,128)S(1)} %bitcast_divide_fusion.2, f32[512]{0:T(512)S(1)} %bitcast.71, f32[1024]{0:T(1024)S(1)} %bitcast.65, f32[512]{0:T(512)S(1)} %bitcast.74, f32[1024]{0:T(1024)S(1)} %bitcast.62, ...), kind=kOutput, calls=%fused_computation.7.clone.1 | convolution fusion | flops 39845888 | bytes 2279424 | tf_op jit(solution)/shard_map/while/body/eval_jaxpr/dot_general | solution.py:102
  224.9 8.5 %convolution_bitcast_fusion.4 = f32[32,1024]{1,0:T(8,128)S(1)} fusion(bf16[32,512]{1,0:T(8,128)(2,1)S(1)} %get-tuple-element.270, f32[1024,512]{1,0:T(8,128)S(1)} %bitcast_divide_fusion.2, f32[512]{0:T(512)S(1)} %bitcast.72, f32[1024]{0:T(1024)S(1)} %bitcast.66, f32[512]{0:T(512)S(1)} %bitcast.75, f32[1024]{0:T(1024)S(1)} %bitcast.63, ...), kind=kOutput, calls=%fused_computation.6.clone.1 | convolution fusion | flops 39845888 | bytes 2279424 | tf_op jit(solution)/shard_map/while/body/eval_jaxpr/dot_general | solution.py:105
  234.9 1.4 bitcast_divide_fusion.2
  236.3 8.4 %convolution_bitcast_fusion.5 = f32[32,1024]{1,0:T(8,128)S(1)} fusion(bf16[32,512]{1,0:T(8,128)(2,1)S(1)} %get-tuple-element.270, f32[1024,512]{1,0:T(8,128)S(1)} %bitcast_divide_fusion.2, f32[512]{0:T(512)S(1)} %bitcast.71, f32[1024]{0:T(1024)S(1)} %bitcast.65, f32[512]{0:T(512)S(1)} %bitcast.74, f32[1024]{0:T(1024)S(1)} %bitcast.62, ...), kind=kOutput, calls=%fused_computation.7.clone.1 | convolution fusion | flops 39845888 | bytes 2279424 | tf_op jit(solution)/shard_map/while/body/eval_jaxpr/dot_general | solution.py:102
  244.7 8.5 %convolution_bitcast_fusion.4 = f32[32,1024]{1,0:T(8,128)S(1)} fusion(bf16[32,512]{1,0:T(8,128)(2,1)S(1)} %get-tuple-element.270, f32[1024,512]{1,0:T(8,128)S(1)} %bitcast_divide_fusion.2, f32[512]{0:T(512)S(1)} %bitcast.72, f32[1024]{0:T(1024)S(1)} %bitcast.66, f32[512]{0:T(512)S(1)} %bitcast.75, f32[1024]{0:T(1024)S(1)} %bitcast.63, ...), kind=kOutput, calls=%fused_computation.6.clone.1 | convolution fusion | flops 39845888 | bytes 2279424 | tf_op jit(solution)/shard_map/while/body/eval_jaxpr/dot_general | solution.py:105
  253.3 1.0 copy-done.1
  254.3 268.1 %reduce-scatter.2.cloned.1.call-done = f32[32,128]{1,0:T(8,128)} async-done(((f32[32,8192]{1,0:T(8,128)}), f32[32,128]{1,0:T(8,128)}) %reduce-scatter.2.cloned.1.call-update) | async-done | bytes 16400 | tf_op jit(solution)/shard_map/reduce_scatter | solution.py:115
  523.2 1.4 scatter_custom_fusion
  (111 shorter events, 21.3 us)
Async XLA Ops:
  8.2 34.2 %collective-permute-start.1 = (f32[32,1,8,128]{3,2,1,0:T(8,128)S(1)}, f32[32,1,8,128]{3,2,1,0:T(8,128)S(1)}, u32[]{:S(2)}, u32[]{:S(2)}) collective-permute-start(f32[32,1,8,128]{3,2,1,0:T(8,128)S(1)} %get-tuple-element.180), channel_id=1, source_target_pairs={{0,16},{16,32},{32,48},{48,64},{64,80},{80,96},{96,112},{112,128},... | collective-permute-start | bytes 393224 | tf_op jit(solution)/shard_map/ppermute | solution.py:26
  9.9 32.5 %collective-permute-start = (f32[32,1,8,128]{3,2,1,0:T(8,128)S(1)}, f32[32,1,8,128]{3,2,1,0:T(8,128)S(1)}, u32[]{:S(2)}, u32[]{:S(2)}) collective-permute-start(f32[32,1,8,128]{3,2,1,0:T(8,128)S(1)} %get-tuple-element.179), channel_id=1, source_target_pairs={{16,0},{32,16},{48,32},{64,48},{80,64},{96,80},{112,96},{128,112},... | collective-permute-start | bytes 393224 | tf_op jit(solution)/shard_map/ppermute | solution.py:27
  12.6 81.8 %all-to-all-start = ((f32[64,3,128]{2,1,0:T(4,128)}), f32[64,3,128]{2,1,0:T(4,128)}, u32[]{:S(2)}, u32[]{:S(2)}) async-start(f32[64,3,128]{2,1,0:T(4,128)} %stack.2), calls=%async_computation | async-start | bytes 262144 | tf_op jit(solution)/shard_map/all_to_all | solution.py:83
  28.2 494.2 %reduce-scatter.2.cloned.1.call-start = ((), (), s32[]{:S(2)}) async-start(), calls=%async_computation.2 | async-start | bytes 1064960 | tf_op jit(solution)/shard_map/reduce_scatter | solution.py:115
  30.2 27.9 %copy-start.9 = (s32[128]{0:T(128)}, s32[128]{0:T(128)S(1)}, u32[]{:S(2)}) copy-start(s32[128]{0:T(128)S(1)} %compare_select_fusion) | copy-start | bytes 1540
  31.4 11.0 %copy-start = (f32[32,2,8,128]{3,2,1,0:T(8,128)S(1)}, f32[32,2,8,128]{3,2,1,0:T(8,128)}, u32[]{:S(2)}) copy-start(f32[32,2,8,128]{3,2,1,0:T(8,128)} %param.9) | copy-start | bytes 786436
  43.4 9.2 %collective-permute-start.2 = (f32[32,4,1,128]{3,0,2,1:T(8,128)S(1)}, f32[32,4,1,128]{3,0,2,1:T(8,128)S(1)}, u32[]{:S(2)}, u32[]{:S(2)}) collective-permute-start(f32[32,4,1,128]{3,0,2,1:T(8,128)S(1)} %copy.91), channel_id=1, source_target_pairs={{4,0},{8,4},{12,8},{5,1},{9,5},{13,9},{6,2},{10,6},{14,10},{7,3},{... | collective-permute-start | bytes 196616 | tf_op jit(solution)/shard_map/ppermute | solution.py:27
  44.7 8.0 %collective-permute-start.3 = (f32[32,4,1,128]{3,0,2,1:T(8,128)S(1)}, f32[32,4,1,128]{3,0,2,1:T(8,128)S(1)}, u32[]{:S(2)}, u32[]{:S(2)}) collective-permute-start(f32[32,4,1,128]{3,0,2,1:T(8,128)S(1)} %copy.92), channel_id=1, source_target_pairs={{0,4},{4,8},{8,12},{1,5},{5,9},{9,13},{2,6},{6,10},{10,14},{3,7},{... | collective-permute-start | bytes 196616 | tf_op jit(solution)/shard_map/ppermute | solution.py:26
  52.7 5.4 %copy-start.2 = (f32[32,4,1,128]{0,2,3,1:T(1,128)}, f32[32,4,1,128]{0,2,3,1:T(1,128)S(1)}, u32[]{:S(2)}) copy-start(f32[32,4,1,128]{0,2,3,1:T(1,128)S(1)} %copy.71) | copy-start | bytes 196612
  52.9 5.3 copy-start.3
  53.6 22.2 %collective-permute-start.4 = (f32[32,4,10,1]{0,2,3,1:T(8,128)}, f32[32,4,10,1]{0,2,3,1:T(8,128)}, u32[]{:S(2)}, u32[]{:S(2)}) collective-permute-start(f32[32,4,10,1]{0,2,3,1:T(8,128)} %get-tuple-element.170), channel_id=1, source_target_pairs={{1,0},{2,1},{3,2},{5,4},{6,5},{7,6},{9,8},{10,9},{11,10},{13,12},{... | collective-permute-start | bytes 15368 | tf_op jit(solution)/shard_map/ppermute | solution.py:27
  56.8 19.0 %collective-permute-start.5 = (f32[32,4,10,1]{0,2,3,1:T(8,128)}, f32[32,4,10,1]{0,2,3,1:T(8,128)}, u32[]{:S(2)}, u32[]{:S(2)}) collective-permute-start(f32[32,4,10,1]{0,2,3,1:T(8,128)} %get-tuple-element.171), channel_id=1, source_target_pairs={{0,1},{1,2},{2,3},{4,5},{5,6},{6,7},{8,9},{9,10},{10,11},{12,13},{... | collective-permute-start | bytes 15368 | tf_op jit(solution)/shard_map/ppermute | solution.py:26
  75.8 2.9 copy-start.4
  79.9 1.0 copy-start.5
  80.0 0.9 copy-start.6
  80.3 1.8 copy-start.7
  80.3 1.8 copy-start.8
  253.3 1.0 copy-start.1
Sparse Core Ops, SparseCore 0:
  254.5 267.9 reduce-scatter.1
